TPU v7x, 512 devices: a whole 4x4x16 slice. The times are simulated.
512 devices in a mesh: gy: 16 (over z), gx: 32 (over x, y, core).
Axes of the slice: x: 4, y: 4, z: 16, core: 2. Of those that a mesh axis runs over, the one named last changes fastest.
Arguments:
- observed: float32 [16, 512, 4096], P(None, 'gy', 'gx'), may hold values from 0 to 20, as said below
- profiles: float32 [64, 3, 9], replicated, may hold values from 0.03 to 0.25
- tile_index: int32 [16, 32], replicated, may hold values from 0 to 63
Outputs:
- estimate: float32 [16, 512, 4096], P(None, 'gy', 'gx')
Inputs may be any that keep to these rules, and one draw needn't show every extreme that they name: `observed`: nonnegative intensities.
All inputs are finite; a program needn't handle non-finite values.
Results may differ from a plain program's by a relative error of at most 0.0003.
Values sent between devices are 32-bit elements; how exact they have to be, the bound alone decides.
A program may use at most 64 MiB of HBM per device.

v0:
```python
import jax
import jax.numpy as jnp
from jax import lax
from jax.sharding import PartitionSpec as P

ITERS = 2
WEIGHT_TV = 0.02
SMOOTHING = 0.1
DAMPING = 0.05
START_STEP = 0.5
EXACT_MODE = lax.Precision.HIGHEST


def extended(block, sides, width):
    for axis, dim in sides:
        count = lax.axis_size(axis)
        forward = [(i, i + 1) for i in range(count - 1)]
        backward = [(target, source) for source, target in forward]
        low = lax.ppermute(
            lax.slice_in_dim(block, block.shape[dim] - width, None, axis=dim), axis, forward
        )
        high = lax.ppermute(lax.slice_in_dim(block, 0, width, axis=dim), axis, backward)
        block = jnp.concatenate([low, block, high], axis=dim)
    return block


def from_behind(block, axis, distance):
    devices = range(lax.axis_size(axis))
    route = [(i - distance, i) for i in devices if i - distance in devices]
    return lax.ppermute(block, axis, route)


def band_matrix(profile, source_start, source_len, target_start, target_len, transposed):
    radius = (profile.shape[0] - 1) // 2
    source = jnp.arange(source_len)[:, None] + source_start
    target = jnp.arange(target_len)[None, :] + target_start
    distance = source - target if transposed else target - source
    offsets = jnp.arange(profile.shape[0]) - radius
    return jnp.sum(jnp.where(distance[:, :, None] == offsets, profile, 0.0), axis=2)


def apply_kernel(
    region, kernel, row_start, col_start, out_rows, out_cols, row_target, col_target, transposed
):
    layers, height, breadth = region.shape
    mix_cols = band_matrix(kernel[2], col_start, breadth, col_target, out_cols, transposed)
    along_cols = jnp.dot(
        region.reshape(layers * height, breadth), mix_cols, precision=EXACT_MODE
    ).reshape(layers, height, out_cols)
    mix_rows = band_matrix(kernel[1], row_start, height, row_target, out_rows, transposed)
    along_rows = jnp.einsum("zyx,yo->zox", along_cols, mix_rows, precision=EXACT_MODE)
    mix_depth = band_matrix(kernel[0], 0, layers, 0, layers, transposed)
    return jnp.einsum("zyx,zo->oyx", along_rows, mix_depth, precision=EXACT_MODE)


def pick_kernel(profiles, tile_index, row_pick, col_pick):
    grid_rows, grid_cols = tile_index.shape
    chosen_tile = (jnp.arange(grid_rows)[:, None] == row_pick) & (
        jnp.arange(grid_cols)[None, :] == col_pick
    )
    kernel_number = jnp.sum(jnp.where(chosen_tile, tile_index, 0))
    chosen_kernel = jnp.arange(profiles.shape[0])[:, None, None] == kernel_number
    return jnp.sum(jnp.where(chosen_kernel, profiles, 0.0), axis=0)


def variation_slope(padded, radius, first_row, first_col, total_rows, total_cols):
    height = padded.shape[1] - 2 * radius
    breadth = padded.shape[2] - 2 * radius
    window = padded[:, radius - 1 : radius + height + 1, radius - 1 : radius + breadth + 1]
    core = window[:, : height + 1, : breadth + 1]
    diff_rows = (window[:, 1:, :] - window[:, :-1, :])[:, :, : breadth + 1]
    diff_cols = (window[:, :, 1:] - window[:, :, :-1])[:, : height + 1, :]
    diff_depth = jnp.concatenate([core[1:] - core[:-1], jnp.zeros_like(core[:1])], 0)
    global_rows = first_row - 1 + jnp.arange(height + 1)
    global_cols = first_col - 1 + jnp.arange(breadth + 1)
    diff_rows = jnp.where((global_rows == total_rows - 1)[:, None], 0.0, diff_rows)
    diff_cols = jnp.where((global_cols == total_cols - 1)[None, :], 0.0, diff_cols)
    magnitude = jnp.sqrt(
        diff_depth * diff_depth
        + diff_rows * diff_rows
        + diff_cols * diff_cols
        + SMOOTHING * SMOOTHING
    )
    inside = (global_rows >= 0)[:, None] & (global_cols >= 0)[None, :]
    flux_rows = jnp.where(inside, diff_rows / magnitude, 0.0)
    flux_cols = jnp.where(inside, diff_cols / magnitude, 0.0)
    flux_depth = jnp.where(inside, diff_depth / magnitude, 0.0)[:, 1:, 1:]
    result = flux_rows[:, :-1, 1:] - flux_rows[:, 1:, 1:]
    result = result + flux_cols[:, 1:, :-1] - flux_cols[:, 1:, 1:]
    depth_before = jnp.concatenate([jnp.zeros_like(flux_depth[:1]), flux_depth[:-1]], 0)
    return result + depth_before - flux_depth


def per_device(observed, profiles, tile_index):
    layers, height, breadth = observed.shape
    radius = (profiles.shape[2] - 1) // 2
    row_number = lax.axis_index("gy")
    col_number = lax.axis_index("gx")
    first_row = row_number * height
    first_col = col_number * breadth
    total_rows = lax.axis_size("gy") * height
    total_cols = lax.axis_size("gx") * breadth
    kernel = pick_kernel(profiles, tile_index, row_number, col_number)

    def slope_at(estimate):
        padded = extended(estimate, (("gy", 1), ("gx", 2)), radius)
        blurred = apply_kernel(padded, kernel, 0, 0, height, breadth, radius, radius, False)
        residual = blurred - observed
        spread = apply_kernel(
            residual, kernel, radius, radius, height + 2 * radius, breadth + 2 * radius, 0, 0, True
        )
        from_right = from_behind(spread[:, :, :radius], "gx", -1)
        from_left = from_behind(spread[:, :, breadth + radius :], "gx", 1)
        middle = spread[:, :, radius : breadth + radius]
        middle = (
            middle.at[:, :, :radius].add(from_left).at[:, :, breadth - radius :].add(from_right)
        )
        from_below = from_behind(middle[:, :radius], "gy", -1)
        from_above = from_behind(middle[:, height + radius :], "gy", 1)
        pulled = (
            middle[:, radius : height + radius]
            .at[:, :radius]
            .add(from_above)
            .at[:, height - radius :]
            .add(from_below)
        )
        smooth = variation_slope(padded, radius, first_row, first_col, total_rows, total_cols)
        return pulled + WEIGHT_TV * smooth + DAMPING * estimate

    previous = observed
    prev_descent = slope_at(previous)
    current = previous - START_STEP * prev_descent
    for iteration in range(ITERS):
        descent = slope_at(current)
        change = current - previous
        growth = descent - prev_descent
        change_sq, change_growth = lax.psum(
            (jnp.sum(change * change), jnp.sum(change * growth)), ("gy", "gx")
        )
        step_size = change_sq / change_growth
        previous, prev_descent = (current, descent)
        current = current - step_size * descent
    return current


def solution(mesh):
    in_specs = (P(None, "gy", "gx"), P(), P())
    out_specs = P(None, "gy", "gx")
    return jax.shard_map(
        per_device, mesh=mesh, in_specs=in_specs, out_specs=out_specs, check_vma=False
    )
```

profile of v0, /device:TPU:1, one launch (start us, length us, event | category | flops | bytes accessed | tf_op | source)
XLA Modules:
  0.0 398.4 jit_solution(11025380353578500066)
XLA Ops:
  0.0 0.9 fusion.81
  0.9 4.4 %collective-permute-start = (f32[16,4,128]{2,1,0:T(4,128)S(1)}, f32[16,4,128]{2,1,0:T(4,128)S(1)}, u32[]{:S(2)}, u32[]{:S(2)}) collective-permute-start(f32[16,4,128]{2,1,0:T(4,128)S(1)} %get-tuple-element.209), channel_id=1, source_target_pairs={{0,32},{32,64},{64,96},{96,128},{128,160},{160,192},{192,224},{224... | collective-permute-start | bytes 98312 | tf_op jit(solution)/shard_map/ppermute | solution.py:19
  5.3 1.3 collective-permute-start.1
  10.3 5.0 %collective-permute-start.2 = (f32[16,40,4]{2,1,0:T(8,128)S(1)}, f32[16,40,4]{2,1,0:T(8,128)S(1)}, u32[]{:S(2)}, u32[]{:S(2)}) collective-permute-start(f32[16,40,4]{2,1,0:T(8,128)S(1)} %get-tuple-element.203), channel_id=1, source_target_pairs={{0,1},{1,2},{2,3},{3,4},{4,5},{5,6},{6,7},{7,8},{8,9},{9,10},{10,1... | collective-permute-start | bytes 30728 | tf_op jit(solution)/shard_map/ppermute | solution.py:19
  15.4 2.9 collective-permute-start.3
  18.4 0.9 collective-permute-done.2
  20.3 3.6 collective-permute-done.3
  26.9 0.7 convolution_bitcast_fusion.2
  27.6 0.8 fusion.10
  28.7 0.8 copy.87
  29.7 1.9 collective-permute-start.4
  31.6 2.4 collective-permute-start.5
  35.6 0.9 copy_add_fusion.2
  36.5 3.6 scatter-add.40
  40.3 1.9 slice_add_fusion.2
  42.2 5.7 %scatter-add.41 = f32[16,40,128]{2,1,0:T(8,128)S(1)} dynamic-update-slice(f32[16,40,128]{2,1,0:T(8,128)S(1)} %scatter-add.40, f32[16,40,4]{2,1,0:T(8,128)} %slice_add_fusion.2, s32[]{:T(128)} %constant.298.clone.1, s32[]{:T(128)} %constant.298.clone.1, s32[]{:T(128)} %constant.301.clone.1) | dynamic-update-slice | bytes 20484 | tf_op jit(solution)/shard_map/scatter-add | solution.py:116
  47.9 3.5 collective-permute-start.6
  52.0 1.3 collective-permute-start.7
  53.3 4.6 %collective-permute-done.7 = f32[16,4,128]{2,1,0:T(4,128)S(1)} collective-permute-done((f32[16,4,128]{2,1,0:T(4,128)S(1)}, f32[16,4,128]{2,1,0:T(4,128)S(1)}, u32[]{:S(2)}, u32[]{:S(2)}) %collective-permute-start.7) | collective-permute-done | bytes 32800 | tf_op jit(solution)/shard_map/ppermute | solution.py:30
  57.9 1.1 multiply_subtract_fusion.2
  59.1 4.8 %collective-permute-start.8 = (f32[16,4,128]{2,1,0:T(4,128)S(1)}, f32[16,4,128]{2,1,0:T(4,128)S(1)}, u32[]{:S(2)}, u32[]{:S(2)}) collective-permute-start(f32[16,4,128]{2,1,0:T(4,128)S(1)} %get-tuple-element.207), channel_id=1, source_target_pairs={{0,32},{32,64},{64,96},{96,128},{128,160},{160,192},{192,224},{224... | collective-permute-start | bytes 98312 | tf_op jit(solution)/shard_map/ppermute | solution.py:19
  63.9 1.3 collective-permute-start.9
  65.2 3.4 collective-permute-done.9
  68.8 6.7 %collective-permute-start.10 = (f32[16,40,4]{2,1,0:T(8,128)S(1)}, f32[16,40,4]{2,1,0:T(8,128)S(1)}, u32[]{:S(2)}, u32[]{:S(2)}) collective-permute-start(f32[16,40,4]{2,1,0:T(8,128)S(1)} %get-tuple-element.199), channel_id=1, source_target_pairs={{0,1},{1,2},{2,3},{3,4},{4,5},{5,6},{6,7},{7,8},{8,9},{9,10},{10,1... | collective-permute-start | bytes 30728 | tf_op jit(solution)/shard_map/ppermute | solution.py:19
  75.5 2.1 collective-permute-start.11
  77.6 1.9 collective-permute-done.10
  80.5 3.4 collective-permute-done.11
  88.0 0.7 convolution_bitcast_fusion.1
  88.8 0.8 fusion.8
  89.8 0.8 copy.91
  90.8 1.9 collective-permute-start.12
  92.7 2.4 collective-permute-start.13
  95.8 1.4 divide_select_fusion.5
  97.6 3.5 scatter-add.46
  101.5 1.1 slice_add_fusion.1
  102.7 5.7 %scatter-add.49 = f32[16,40,128]{2,1,0:T(8,128)S(1)} dynamic-update-slice(f32[16,40,128]{2,1,0:T(8,128)S(1)} %scatter-add.46, f32[16,40,4]{2,1,0:T(8,128)S(1)} %slice_add_fusion.1, s32[]{:T(128)} %constant.298.clone.1, s32[]{:T(128)} %constant.298.clone.1, s32[]{:T(128)} %constant.301.clone.1) | dynamic-update-slice | bytes 20484 | tf_op jit(solution)/shard_map/scatter-add | solution.py:116
  108.4 4.1 %collective-permute-start.14 = (f32[16,4,128]{2,1,0:T(4,128)S(1)}, f32[16,4,128]{2,1,0:T(4,128)S(1)}, u32[]{:S(2)}, u32[]{:S(2)}) collective-permute-start(f32[16,4,128]{2,1,0:T(4,128)S(1)} %get-tuple-element.198), channel_id=1, source_target_pairs={{0,32},{32,64},{64,96},{96,128},{128,160},{160,192},{192,224},{224... | collective-permute-start | bytes 98312 | tf_op jit(solution)/shard_map/ppermute | solution.py:30
  113.0 1.4 collective-permute-start.15
  114.4 3.6 collective-permute-done.15
  118.1 1.1 multiply_reduce_fusion.2
  119.2 113.8 %all-reduce.7 = (f32[]{:T(128)}, f32[]{:T(128)}) all-reduce(f32[]{:T(128)} %get-tuple-element.152, f32[]{:T(128)} %get-tuple-element.151), channel_id=1, replica_groups=mesh['gy'=16,'gx'=32] {'gy','gx'}, use_global_device_ids=true, to_apply=%region_9.10 | all-reduce | flops 2 | bytes 16 | tf_op jit(solution)/shard_map/psum | solution.py:137
  234.3 1.3 collective-permute-start.16
  235.6 1.3 collective-permute-start.17
  236.9 3.3 collective-permute-done.17
  240.5 3.8 collective-permute-start.18
  244.3 2.1 collective-permute-start.19
  246.5 1.8 collective-permute-done.18
  249.3 3.4 collective-permute-done.19
  256.8 0.7 convolution_bitcast_fusion
  257.5 0.8 fusion.6
  258.6 0.8 copy.95
  259.5 1.9 collective-permute-start.20
  261.4 2.4 collective-permute-start.21
  264.5 1.4 divide_select_fusion.2
  266.2 0.9 copy_add_fusion
  267.1 3.6 scatter-add.54
  270.7 1.8 slice_add_fusion
  272.5 5.7 %scatter-add.55 = f32[16,40,128]{2,1,0:T(8,128)S(1)} dynamic-update-slice(f32[16,40,128]{2,1,0:T(8,128)S(1)} %scatter-add.54, f32[16,40,4]{2,1,0:T(8,128)} %slice_add_fusion, s32[]{:T(128)} %constant.298.clone.1, s32[]{:T(128)} %constant.298.clone.1, s32[]{:T(128)} %constant.301.clone.1) | dynamic-update-slice | bytes 20484 | tf_op jit(solution)/shard_map/scatter-add | solution.py:116
  278.3 2.9 collective-permute-start.22
  281.6 1.4 collective-permute-start.23
  283.1 4.0 collective-permute-done.23
  287.1 1.0 multiply_reduce_fusion
  288.2 108.2 %all-reduce.6 = (f32[]{:T(128)}, f32[]{:T(128)}) all-reduce(f32[]{:T(128)} %get-tuple-element.150, f32[]{:T(128)} %get-tuple-element.149), channel_id=1, replica_groups=mesh['gy'=16,'gx'=32] {'gy','gx'}, use_global_device_ids=true, to_apply=%region_13.14 | all-reduce | flops 2 | bytes 16 | tf_op jit(solution)/shard_map/psum | solution.py:137
  397.7 0.7 multiply_subtract_fusion
  (171 shorter events, 24.7 us)
Async XLA Ops:
  0.9 8.8 %collective-permute-start = (f32[16,4,128]{2,1,0:T(4,128)S(1)}, f32[16,4,128]{2,1,0:T(4,128)S(1)}, u32[]{:S(2)}, u32[]{:S(2)}) collective-permute-start(f32[16,4,128]{2,1,0:T(4,128)S(1)} %get-tuple-element.209), channel_id=1, source_target_pairs={{0,32},{32,64},{64,96},{96,128},{128,160},{160,192},{192,224},{224... | collective-permute-start | bytes 98312 | tf_op jit(solution)/shard_map/ppermute | solution.py:19
  5.3 4.8 %collective-permute-start.1 = (f32[16,4,128]{2,1,0:T(4,128)S(1)}, f32[16,4,128]{2,1,0:T(4,128)S(1)}, u32[]{:S(2)}, u32[]{:S(2)}) collective-permute-start(f32[16,4,128]{2,1,0:T(4,128)S(1)} %get-tuple-element.210), channel_id=1, source_target_pairs={{32,0},{64,32},{96,64},{128,96},{160,128},{192,160},{224,192},{256... | collective-permute-start | bytes 98312 | tf_op jit(solution)/shard_map/ppermute | solution.py:22
  6.7 0.7 copy-start.30
  6.7 2.1 copy-start.25
  6.8 3.3 copy-start
  8.8 25.2 %copy-start.31 = (pred[33]{0:T(512)(128)(4,1)}, pred[33]{0:T(512)(128)(4,1)S(1)}, u32[]{:S(2)}) copy-start(pred[33]{0:T(512)(128)(4,1)S(1)} %get-tuple-element.215) | copy-start | bytes 103
  8.8 42.6 %copy-start.26 = (pred[129]{0:T(512)(128)(4,1)}, pred[129]{0:T(512)(128)(4,1)S(1)}, u32[]{:S(2)}) copy-start(pred[129]{0:T(512)(128)(4,1)S(1)} %get-tuple-element.213) | copy-start | bytes 391
  9.2 16.1 %copy-start.19 = (f32[40,32]{0,1:T(8,128)}, f32[40,32]{0,1:T(8,128)S(1)}, u32[]{:S(2)}) copy-start(f32[40,32]{0,1:T(8,128)S(1)} %select_reduce_fusion.2) | copy-start | bytes 15364
  9.3 17.6 %copy-start.16 = (f32[32,40]{1,0:T(8,128)}, f32[32,40]{1,0:T(8,128)S(1)}, u32[]{:S(2)}) copy-start(f32[32,40]{1,0:T(8,128)S(1)} %select_reduce_fusion.3) | copy-start | bytes 15364
  9.5 16.8 %copy-start.7 = (f32[128,136]{0,1:T(8,128)}, f32[128,136]{0,1:T(8,128)S(1)}, u32[]{:S(2)}) copy-start(f32[128,136]{0,1:T(8,128)S(1)} %select_reduce_fusion) | copy-start | bytes 208900
  9.6 15.0 %copy-start.5 = (f32[136,128]{1,0:T(8,128)}, f32[136,128]{1,0:T(8,128)S(1)}, u32[]{:S(2)}) copy-start(f32[136,128]{1,0:T(8,128)S(1)} %select_reduce_fusion.1) | copy-start | bytes 208900
  10.1 13.7 %copy-start.11 = (f32[16,4,128]{2,1,0:T(4,128)}, f32[16,4,128]{2,1,0:T(4,128)S(1)}, u32[]{:S(2)}) copy-start(f32[16,4,128]{2,1,0:T(4,128)S(1)} %collective-permute-done.1) | copy-start | bytes 98308
  10.3 9.0 %collective-permute-start.2 = (f32[16,40,4]{2,1,0:T(8,128)S(1)}, f32[16,40,4]{2,1,0:T(8,128)S(1)}, u32[]{:S(2)}, u32[]{:S(2)}) collective-permute-start(f32[16,40,4]{2,1,0:T(8,128)S(1)} %get-tuple-element.203), channel_id=1, source_target_pairs={{0,1},{1,2},{2,3},{3,4},{4,5},{5,6},{6,7},{7,8},{8,9},{9,10},{10,1... | collective-permute-start | bytes 30728 | tf_op jit(solution)/shard_map/ppermute | solution.py:19
  15.4 10.3 %copy-start.22 = (f32[16,16]{1,0:T(8,128)}, f32[16,16]{1,0:T(8,128)S(1)}, u32[]{:S(2)}) copy-start(f32[16,16]{1,0:T(8,128)S(1)} %get-tuple-element.157) | copy-start | bytes 3076
  15.4 8.4 %collective-permute-start.3 = (f32[16,40,4]{2,1,0:T(8,128)S(1)}, f32[16,40,4]{2,1,0:T(8,128)S(1)}, u32[]{:S(2)}, u32[]{:S(2)}) collective-permute-start(f32[16,40,4]{2,1,0:T(8,128)S(1)} %get-tuple-element.204), channel_id=1, source_target_pairs={{1,0},{2,1},{3,2},{4,3},{5,4},{6,5},{7,6},{8,7},{9,8},{10,9},{11,1... | collective-permute-start | bytes 30728 | tf_op jit(solution)/shard_map/ppermute | solution.py:22
  29.6 4.5 %copy-start.12 = (f32[16,4,128]{2,1,0:T(4,128)S(1)}, f32[16,4,128]{2,1,0:T(4,128)}, u32[]{:S(2)}) copy-start(f32[16,4,128]{2,1,0:T(4,128)} %copy-done.11) | copy-start | bytes 98308
  29.7 5.9 %collective-permute-start.4 = (f32[16,40,4]{2,1,0:T(8,128)S(1)}, f32[16,40,4]{2,1,0:T(8,128)S(1)}, u32[]{:S(2)}, u32[]{:S(2)}) collective-permute-start(f32[16,40,4]{2,1,0:T(8,128)S(1)} %copy.86), channel_id=1, source_target_pairs={{0,1},{1,2},{2,3},{3,4},{4,5},{5,6},{6,7},{7,8},{8,9},{9,10},{10,1... | collective-permute-start | bytes 30728 | tf_op jit(solution)/shard_map/ppermute | solution.py:30
  31.6 8.7 %collective-permute-start.5 = (f32[16,40,4]{2,1,0:T(8,128)}, f32[16,40,4]{2,1,0:T(8,128)}, u32[]{:S(2)}, u32[]{:S(2)}) collective-permute-start(f32[16,40,4]{2,1,0:T(8,128)} %copy.87), channel_id=1, source_target_pairs={{1,0},{2,1},{3,2},{4,3},{5,4},{6,5},{7,6},{8,7},{9,8},{10,9},{11,1... | collective-permute-start | bytes 30728 | tf_op jit(solution)/shard_map/ppermute | solution.py:30
  47.9 3.6 copy-start.13
  47.9 5.3 %collective-permute-start.6 = (f32[16,4,128]{2,1,0:T(4,128)S(1)}, f32[16,4,128]{2,1,0:T(4,128)S(1)}, u32[]{:S(2)}, u32[]{:S(2)}) collective-permute-start(f32[16,4,128]{2,1,0:T(4,128)S(1)} %get-tuple-element.202), channel_id=1, source_target_pairs={{0,32},{32,64},{64,96},{96,128},{128,160},{160,192},{192,224},{224... | collective-permute-start | bytes 98312 | tf_op jit(solution)/shard_map/ppermute | solution.py:30
  52.0 6.0 %collective-permute-start.7 = (f32[16,4,128]{2,1,0:T(4,128)S(1)}, f32[16,4,128]{2,1,0:T(4,128)S(1)}, u32[]{:S(2)}, u32[]{:S(2)}) collective-permute-start(f32[16,4,128]{2,1,0:T(4,128)S(1)} %get-tuple-element.201), channel_id=1, source_target_pairs={{32,0},{64,32},{96,64},{128,96},{160,128},{192,160},{224,192},{256... | collective-permute-start | bytes 98312 | tf_op jit(solution)/shard_map/ppermute | solution.py:30
  59.1 6.2 %collective-permute-start.8 = (f32[16,4,128]{2,1,0:T(4,128)S(1)}, f32[16,4,128]{2,1,0:T(4,128)S(1)}, u32[]{:S(2)}, u32[]{:S(2)}) collective-permute-start(f32[16,4,128]{2,1,0:T(4,128)S(1)} %get-tuple-element.207), channel_id=1, source_target_pairs={{0,32},{32,64},{64,96},{96,128},{128,160},{160,192},{192,224},{224... | collective-permute-start | bytes 98312 | tf_op jit(solution)/shard_map/ppermute | solution.py:19
  63.9 4.7 %collective-permute-start.9 = (f32[16,4,128]{2,1,0:T(4,128)S(1)}, f32[16,4,128]{2,1,0:T(4,128)S(1)}, u32[]{:S(2)}, u32[]{:S(2)}) collective-permute-start(f32[16,4,128]{2,1,0:T(4,128)S(1)} %get-tuple-element.208), channel_id=1, source_target_pairs={{32,0},{64,32},{96,64},{128,96},{160,128},{192,160},{224,192},{256... | collective-permute-start | bytes 98312 | tf_op jit(solution)/shard_map/ppermute | solution.py:22
  68.6 26.6 %copy-start.14 = (f32[16,4,128]{2,1,0:T(4,128)}, f32[16,4,128]{2,1,0:T(4,128)S(1)}, u32[]{:S(2)}) copy-start(f32[16,4,128]{2,1,0:T(4,128)S(1)} %collective-permute-done.9) | copy-start | bytes 98308
  68.8 10.7 %collective-permute-start.10 = (f32[16,40,4]{2,1,0:T(8,128)S(1)}, f32[16,40,4]{2,1,0:T(8,128)S(1)}, u32[]{:S(2)}, u32[]{:S(2)}) collective-permute-start(f32[16,40,4]{2,1,0:T(8,128)S(1)} %get-tuple-element.199), channel_id=1, source_target_pairs={{0,1},{1,2},{2,3},{3,4},{4,5},{5,6},{6,7},{7,8},{8,9},{9,10},{10,1... | collective-permute-start | bytes 30728 | tf_op jit(solution)/shard_map/ppermute | solution.py:19
  75.5 8.4 %collective-permute-start.11 = (f32[16,40,4]{2,1,0:T(8,128)S(1)}, f32[16,40,4]{2,1,0:T(8,128)S(1)}, u32[]{:S(2)}, u32[]{:S(2)}) collective-permute-start(f32[16,40,4]{2,1,0:T(8,128)S(1)} %get-tuple-element.200), channel_id=1, source_target_pairs={{1,0},{2,1},{3,2},{4,3},{5,4},{6,5},{7,6},{8,7},{9,8},{10,9},{11,1... | collective-permute-start | bytes 30728 | tf_op jit(solution)/shard_map/ppermute | solution.py:22
  80.5 3.9 copy-start.6
  85.0 0.7 copy-start.20
  85.7 0.7 copy-start.23
  86.4 0.9 copy-start.8
  87.3 0.7 copy-start.17
  90.8 6.7 %collective-permute-start.12 = (f32[16,40,4]{2,1,0:T(8,128)S(1)}, f32[16,40,4]{2,1,0:T(8,128)S(1)}, u32[]{:S(2)}, u32[]{:S(2)}) collective-permute-start(f32[16,40,4]{2,1,0:T(8,128)S(1)} %copy.90), channel_id=1, source_target_pairs={{0,1},{1,2},{2,3},{3,4},{4,5},{5,6},{6,7},{7,8},{8,9},{9,10},{10,1... | collective-permute-start | bytes 30728 | tf_op jit(solution)/shard_map/ppermute | solution.py:30
  92.7 8.8 %collective-permute-start.13 = (f32[16,40,4]{2,1,0:T(8,128)}, f32[16,40,4]{2,1,0:T(8,128)}, u32[]{:S(2)}, u32[]{:S(2)}) collective-permute-start(f32[16,40,4]{2,1,0:T(8,128)} %copy.91), channel_id=1, source_target_pairs={{1,0},{2,1},{3,2},{4,3},{5,4},{6,5},{7,6},{8,7},{9,8},{10,9},{11,1... | collective-permute-start | bytes 30728 | tf_op jit(solution)/shard_map/ppermute | solution.py:30
  95.1 0.6 copy-start.27
  95.2 0.6 copy-start.32
  108.3 4.1 %copy-start.15 = (f32[16,4,128]{2,1,0:T(4,128)S(1)}, f32[16,4,128]{2,1,0:T(4,128)}, u32[]{:S(2)}) copy-start(f32[16,4,128]{2,1,0:T(4,128)} %copy-done.14) | copy-start | bytes 98308
  108.4 4.1 %copy-start.28 = (pred[129]{0:T(512)(128)(4,1)S(1)}, pred[129]{0:T(512)(128)(4,1)}, u32[]{:S(2)}) copy-start(pred[129]{0:T(512)(128)(4,1)} %copy-done.26) | copy-start | bytes 391
  108.4 6.0 %collective-permute-start.14 = (f32[16,4,128]{2,1,0:T(4,128)S(1)}, f32[16,4,128]{2,1,0:T(4,128)S(1)}, u32[]{:S(2)}, u32[]{:S(2)}) collective-permute-start(f32[16,4,128]{2,1,0:T(4,128)S(1)} %get-tuple-element.198), channel_id=1, source_target_pairs={{0,32},{32,64},{64,96},{96,128},{128,160},{160,192},{192,224},{224... | collective-permute-start | bytes 98312 | tf_op jit(solution)/shard_map/ppermute | solution.py:30
  112.8 5.3 %copy-start.4 = (f32[16,33,129]{2,1,0:T(8,128)S(1)}, f32[16,33,129]{2,1,0:T(8,128)}, u32[]{:S(2)}) copy-start(f32[16,33,129]{2,1,0:T(8,128)} %get-tuple-element.166) | copy-start | bytes 817348
  112.9 5.2 %copy-start.10 = (f32[16,32,128]{2,1,0:T(8,128)S(1)}, f32[16,32,128]{2,1,0:T(8,128)}, u32[]{:S(2)}) copy-start(f32[16,32,128]{2,1,0:T(8,128)} %get-tuple-element.169) | copy-start | bytes 786436
  113.0 5.1 %collective-permute-start.15 = (f32[16,4,128]{2,1,0:T(4,128)S(1)}, f32[16,4,128]{2,1,0:T(4,128)S(1)}, u32[]{:S(2)}, u32[]{:S(2)}) collective-permute-start(f32[16,4,128]{2,1,0:T(4,128)S(1)} %get-tuple-element.197), channel_id=1, source_target_pairs={{32,0},{64,32},{96,64},{128,96},{160,128},{192,160},{224,192},{256... | collective-permute-start | bytes 98312 | tf_op jit(solution)/shard_map/ppermute | solution.py:30
  119.2 115.1 %copy-start.1 = (f32[16,32,128]{2,1,0:T(8,128)}, f32[16,32,128]{2,1,0:T(8,128)S(1)}, u32[]{:S(2)}) copy-start(f32[16,32,128]{2,1,0:T(8,128)S(1)} %get-tuple-element.165) | copy-start | bytes 786436
  234.3 2.6 collective-permute-start.16
  235.6 4.7 %collective-permute-start.17 = (f32[16,4,128]{2,1,0:T(4,128)S(1)}, f32[16,4,128]{2,1,0:T(4,128)S(1)}, u32[]{:S(2)}, u32[]{:S(2)}) collective-permute-start(f32[16,4,128]{2,1,0:T(4,128)S(1)} %get-tuple-element.206), channel_id=1, source_target_pairs={{32,0},{64,32},{96,64},{128,96},{160,128},{192,160},{224,192},{256... | collective-permute-start | bytes 98312 | tf_op jit(solution)/shard_map/ppermute | solution.py:22
  240.5 7.8 %collective-permute-start.18 = (f32[16,40,4]{2,1,0:T(8,128)S(1)}, f32[16,40,4]{2,1,0:T(8,128)S(1)}, u32[]{:S(2)}, u32[]{:S(2)}) collective-permute-start(f32[16,40,4]{2,1,0:T(8,128)S(1)} %get-tuple-element.195), channel_id=1, source_target_pairs={{0,1},{1,2},{2,3},{3,4},{4,5},{5,6},{6,7},{7,8},{8,9},{9,10},{10,1... | collective-permute-start | bytes 30728 | tf_op jit(solution)/shard_map/ppermute | solution.py:19
  244.3 8.4 %collective-permute-start.19 = (f32[16,40,4]{2,1,0:T(8,128)S(1)}, f32[16,40,4]{2,1,0:T(8,128)S(1)}, u32[]{:S(2)}, u32[]{:S(2)}) collective-permute-start(f32[16,40,4]{2,1,0:T(8,128)S(1)} %get-tuple-element.196), channel_id=1, source_target_pairs={{1,0},{2,1},{3,2},{4,3},{5,4},{6,5},{7,6},{8,7},{9,8},{10,9},{11,1... | collective-permute-start | bytes 30728 | tf_op jit(solution)/shard_map/ppermute | solution.py:22
  253.8 0.7 copy-start.21
  254.5 0.7 copy-start.24
  255.2 0.9 copy-start.9
  256.1 0.7 copy-start.18
  259.5 6.7 %collective-permute-start.20 = (f32[16,40,4]{2,1,0:T(8,128)S(1)}, f32[16,40,4]{2,1,0:T(8,128)S(1)}, u32[]{:S(2)}, u32[]{:S(2)}) collective-permute-start(f32[16,40,4]{2,1,0:T(8,128)S(1)} %copy.94), channel_id=1, source_target_pairs={{0,1},{1,2},{2,3},{3,4},{4,5},{5,6},{6,7},{7,8},{8,9},{9,10},{10,1... | collective-permute-start | bytes 30728 | tf_op jit(solution)/shard_map/ppermute | solution.py:30
  261.4 9.2 %collective-permute-start.21 = (f32[16,40,4]{2,1,0:T(8,128)}, f32[16,40,4]{2,1,0:T(8,128)}, u32[]{:S(2)}, u32[]{:S(2)}) collective-permute-start(f32[16,40,4]{2,1,0:T(8,128)} %copy.95), channel_id=1, source_target_pairs={{1,0},{2,1},{3,2},{4,3},{5,4},{6,5},{7,6},{8,7},{9,8},{10,9},{11,1... | collective-permute-start | bytes 30728 | tf_op jit(solution)/shard_map/ppermute | solution.py:30
  263.9 0.6 copy-start.29
  263.9 0.6 copy-start.33
  278.3 4.8 %collective-permute-start.22 = (f32[16,4,128]{2,1,0:T(4,128)S(1)}, f32[16,4,128]{2,1,0:T(4,128)S(1)}, u32[]{:S(2)}, u32[]{:S(2)}) collective-permute-start(f32[16,4,128]{2,1,0:T(4,128)S(1)} %get-tuple-element.194), channel_id=1, source_target_pairs={{0,32},{32,64},{64,96},{96,128},{128,160},{160,192},{192,224},{224... | collective-permute-start | bytes 98312 | tf_op jit(solution)/shard_map/ppermute | solution.py:30
  281.4 5.6 %copy-start.3 = (f32[16,33,129]{2,1,0:T(8,128)S(1)}, f32[16,33,129]{2,1,0:T(8,128)}, u32[]{:S(2)}) copy-start(f32[16,33,129]{2,1,0:T(8,128)} %get-tuple-element.163) | copy-start | bytes 817348
  281.6 5.5 %copy-start.2 = (f32[16,32,128]{2,1,0:T(8,128)S(1)}, f32[16,32,128]{2,1,0:T(8,128)}, u32[]{:S(2)}) copy-start(f32[16,32,128]{2,1,0:T(8,128)} %copy-done.1) | copy-start | bytes 786436
  281.6 5.4 %collective-permute-start.23 = (f32[16,4,128]{2,1,0:T(4,128)S(1)}, f32[16,4,128]{2,1,0:T(4,128)S(1)}, u32[]{:S(2)}, u32[]{:S(2)}) collective-permute-start(f32[16,4,128]{2,1,0:T(4,128)S(1)} %get-tuple-element.193), channel_id=1, source_target_pairs={{32,0},{64,32},{96,64},{128,96},{160,128},{192,160},{224,192},{256... | collective-permute-start | bytes 98312 | tf_op jit(solution)/shard_map/ppermute | solution.py:30
where the time goes:
time: 400 us; the launch traced here: 398 us
  blocking collectives  222 us (56%)
  starting transfers between devices  64.8 us (16%)
  local copies, waits for them, and re-layouts  40.1 us (10%)
  waiting for transfers between devices  35.8 us (9%)
  other arithmetic  20.8 us (5%)
  matrix products  11.2 us (3%)
    psum x2, blocking collectives, per_device(): lax.psum((jnp.sum(change * change), jnp.sum(change * growth)), ('gy', 'gx'))  222 us
    scatter-add x6, local copies, waits for them, and re-layouts, slope_at(): middle.at[:, :, :radius].add(from_left).at[:, :, breadth - radius:]  27.7 us
    ppermute x12, starting transfers between devices, from_behind(): return lax.ppermute(block, axis, route)  27.7 us
    ppermute x6, starting transfers between devices, extended(): lax.ppermute(lax.slice_in_dim(block, block.shape[dim] - width, None, axis...  26.1 us
    ppermute x6, waiting for transfers between devices, extended(): lax.ppermute(lax.slice_in_dim(block, 0, width, axis=dim), axis, backward)  17.5 us
    ppermute x12, waiting for transfers between devices, from_behind(): return lax.ppermute(block, axis, route)  13.6 us
    ppermute x6, starting transfers between devices, extended(): lax.ppermute(lax.slice_in_dim(block, 0, width, axis=dim), axis, backward)  11.1 us
  transfers between devices with their start and end apart: 24, of which 15 were waited for; matrix products, arithmetic and copies ran while one was open for 6% of the time, Pallas kernels for 0%

commit v1 on v0

--- a/solution.py
+++ b/solution.py
@@ -2,6 +2,7 @@
 import jax.numpy as jnp
 from jax import lax
 from jax.sharding import PartitionSpec as P
+from jax.lax import psum
 
 ITERS = 2
 WEIGHT_TV = 0.02
@@ -9,6 +10,12 @@
 DAMPING = 0.05
 START_STEP = 0.5
 EXACT_MODE = lax.Precision.HIGHEST
+
+
+def loads_wait(x_local, axis_tag, axis_key):
+    for d in (axis_tag, axis_key):
+        x_local = psum(x_local, d)
+    return x_local
 
 
 def extended(block, sides, width):
@@ -134,8 +141,8 @@
         descent = slope_at(current)
         change = current - previous
         growth = descent - prev_descent
-        change_sq, change_growth = lax.psum(
-            (jnp.sum(change * change), jnp.sum(change * growth)), ("gy", "gx")
+        change_sq, change_growth = loads_wait(
+            (jnp.sum(change * change), jnp.sum(change * growth)), "gy", "gx"
         )
         step_size = change_sq / change_growth
         previous, prev_descent = (current, descent)

time: 400 us -> 368 us (0.920)
  blocking collectives: 222 us -> 191 us
    psum x2 -> x4, blocking collectives: 222 us -> 191 us  [loads_wait(): x_local = psum(x_local, d)]
where the time goes in v1:
time: 368 us; the launch traced here: 366 us
  blocking collectives  191 us (52%)
  starting transfers between devices  64.1 us (17%)
  local copies, waits for them, and re-layouts  40.2 us (11%)
  waiting for transfers between devices  35.9 us (10%)
  other arithmetic  20.6 us (6%)
  matrix products  11.2 us (3%)
    psum x4, blocking collectives, loads_wait(): x_local = psum(x_local, d)  191 us
    ppermute x12, starting transfers between devices, from_behind(): return lax.ppermute(block, axis, route)  28.2 us
    scatter-add x6, local copies, waits for them, and re-layouts, slope_at(): middle.at[:, :, :radius].add(from_left).at[:, :, breadth - radius:]  27.7 us
    ppermute x6, starting transfers between devices, extended(): lax.ppermute(lax.slice_in_dim(block, block.shape[dim] - width, None, axis...  24.2 us
    ppermute x6, waiting for transfers between devices, extended(): lax.ppermute(lax.slice_in_dim(block, 0, width, axis=dim), axis, backward)  17.7 us
    ppermute x12, waiting for transfers between devices, from_behind(): return lax.ppermute(block, axis, route)  14.2 us
    ppermute x6, starting transfers between devices, extended(): lax.ppermute(lax.slice_in_dim(block, 0, width, axis=dim), axis, backward)  11.8 us
  transfers between devices with their start and end apart: 24, of which 15 were waited for; matrix products, arithmetic and copies ran while one was open for 6% of the time, Pallas kernels for 0%

profile of v1, /device:TPU:1, one launch (start us, length us, event | category | flops | bytes accessed | tf_op | source)
XLA Modules:
  0.0 366.4 jit_solution(15697056504585139599)
XLA Ops:
  0.0 0.9 fusion.81
  0.9 4.4 %collective-permute-start = (f32[16,4,128]{2,1,0:T(4,128)S(1)}, f32[16,4,128]{2,1,0:T(4,128)S(1)}, u32[]{:S(2)}, u32[]{:S(2)}) collective-permute-start(f32[16,4,128]{2,1,0:T(4,128)S(1)} %get-tuple-element.213), channel_id=1, source_target_pairs={{0,32},{32,64},{64,96},{96,128},{128,160},{160,192},{192,224},{224... | collective-permute-start | bytes 98312 | tf_op jit(solution)/shard_map/ppermute | solution.py:26
  5.3 1.3 collective-permute-start.1
  10.3 5.0 %collective-permute-start.2 = (f32[16,40,4]{2,1,0:T(8,128)S(1)}, f32[16,40,4]{2,1,0:T(8,128)S(1)}, u32[]{:S(2)}, u32[]{:S(2)}) collective-permute-start(f32[16,40,4]{2,1,0:T(8,128)S(1)} %get-tuple-element.207), channel_id=1, source_target_pairs={{0,1},{1,2},{2,3},{3,4},{4,5},{5,6},{6,7},{7,8},{8,9},{9,10},{10,1... | collective-permute-start | bytes 30728 | tf_op jit(solution)/shard_map/ppermute | solution.py:26
  15.4 2.9 collective-permute-start.3
  18.4 0.9 collective-permute-done.2
  20.3 3.6 collective-permute-done.3
  27.6 0.8 fusion.10
  28.7 0.8 copy.87
  29.6 1.9 collective-permute-start.4
  31.6 2.4 collective-permute-start.5
  35.6 0.9 copy_add_fusion.2
  36.4 3.6 scatter-add.40
  40.3 1.8 slice_add_fusion.2
  42.1 5.7 %scatter-add.41 = f32[16,40,128]{2,1,0:T(8,128)S(1)} dynamic-update-slice(f32[16,40,128]{2,1,0:T(8,128)S(1)} %scatter-add.40, f32[16,40,4]{2,1,0:T(8,128)} %slice_add_fusion.2, s32[]{:T(128)} %constant.298.clone.1, s32[]{:T(128)} %constant.298.clone.1, s32[]{:T(128)} %constant.301.clone.1) | dynamic-update-slice | bytes 20484 | tf_op jit(solution)/shard_map/scatter-add | solution.py:123
  47.9 3.5 collective-permute-start.6
  51.9 1.3 collective-permute-start.7
  53.2 4.6 %collective-permute-done.7 = f32[16,4,128]{2,1,0:T(4,128)S(1)} collective-permute-done((f32[16,4,128]{2,1,0:T(4,128)S(1)}, f32[16,4,128]{2,1,0:T(4,128)S(1)}, u32[]{:S(2)}, u32[]{:S(2)}) %collective-permute-start.7) | collective-permute-done | bytes 32800 | tf_op jit(solution)/shard_map/ppermute | solution.py:37
  57.9 1.1 multiply_subtract_fusion.2
  59.0 4.8 %collective-permute-start.8 = (f32[16,4,128]{2,1,0:T(4,128)S(1)}, f32[16,4,128]{2,1,0:T(4,128)S(1)}, u32[]{:S(2)}, u32[]{:S(2)}) collective-permute-start(f32[16,4,128]{2,1,0:T(4,128)S(1)} %get-tuple-element.211), channel_id=1, source_target_pairs={{0,32},{32,64},{64,96},{96,128},{128,160},{160,192},{192,224},{224... | collective-permute-start | bytes 98312 | tf_op jit(solution)/shard_map/ppermute | solution.py:26
  63.9 1.3 collective-permute-start.9
  65.2 3.4 collective-permute-done.9
  68.7 6.7 %collective-permute-start.10 = (f32[16,40,4]{2,1,0:T(8,128)S(1)}, f32[16,40,4]{2,1,0:T(8,128)S(1)}, u32[]{:S(2)}, u32[]{:S(2)}) collective-permute-start(f32[16,40,4]{2,1,0:T(8,128)S(1)} %get-tuple-element.203), channel_id=1, source_target_pairs={{0,1},{1,2},{2,3},{3,4},{4,5},{5,6},{6,7},{7,8},{8,9},{9,10},{10,1... | collective-permute-start | bytes 30728 | tf_op jit(solution)/shard_map/ppermute | solution.py:26
  75.5 2.1 collective-permute-start.11
  77.6 1.9 collective-permute-done.10
  80.4 3.4 collective-permute-done.11
  88.0 0.7 convolution_bitcast_fusion.1
  88.7 0.8 fusion.8
  89.8 0.8 copy.91
  90.7 1.9 collective-permute-start.12
  92.7 2.4 collective-permute-start.13
  95.8 1.4 divide_select_fusion.5
  97.6 3.5 scatter-add.46
  101.5 1.1 slice_add_fusion.1
  102.6 5.7 %scatter-add.49 = f32[16,40,128]{2,1,0:T(8,128)S(1)} dynamic-update-slice(f32[16,40,128]{2,1,0:T(8,128)S(1)} %scatter-add.46, f32[16,40,4]{2,1,0:T(8,128)S(1)} %slice_add_fusion.1, s32[]{:T(128)} %constant.298.clone.1, s32[]{:T(128)} %constant.298.clone.1, s32[]{:T(128)} %constant.301.clone.1) | dynamic-update-slice | bytes 20484 | tf_op jit(solution)/shard_map/scatter-add | solution.py:123
  108.3 4.1 %collective-permute-start.14 = (f32[16,4,128]{2,1,0:T(4,128)S(1)}, f32[16,4,128]{2,1,0:T(4,128)S(1)}, u32[]{:S(2)}, u32[]{:S(2)}) collective-permute-start(f32[16,4,128]{2,1,0:T(4,128)S(1)} %get-tuple-element.202), channel_id=1, source_target_pairs={{0,32},{32,64},{64,96},{96,128},{128,160},{160,192},{192,224},{224... | collective-permute-start | bytes 98312 | tf_op jit(solution)/shard_map/ppermute | solution.py:37
  112.9 1.4 collective-permute-start.15
  114.4 3.6 collective-permute-done.15
  118.0 1.1 multiply_reduce_fusion.2
  119.1 25.6 %all-reduce.9 = (f32[]{:T(128)}, f32[]{:T(128)}) all-reduce(f32[]{:T(128)} %get-tuple-element.152, f32[]{:T(128)} %get-tuple-element.151), channel_id=1, replica_groups=mesh['gy'=16,'gx'=32] {'gy'}, use_global_device_ids=true, to_apply=%region_9.10 | all-reduce | flops 2 | bytes 16 | tf_op jit(solution)/shard_map/psum | solution.py:17
  144.7 71.1 %all-reduce.7 = (f32[]{:T(128)}, f32[]{:T(128)}) all-reduce(f32[]{:T(128)} %get-tuple-element.164, f32[]{:T(128)} %get-tuple-element.165), channel_id=1, replica_groups=mesh['gy'=16,'gx'=32] {'gx'}, use_global_device_ids=true, to_apply=%region_10.11 | all-reduce | flops 2 | bytes 16 | tf_op jit(solution)/shard_map/psum | solution.py:17
  217.1 1.3 collective-permute-start.16
  218.4 1.3 collective-permute-start.17
  219.7 3.6 collective-permute-done.17
  223.5 1.9 collective-permute-start.18
  225.4 2.8 collective-permute-start.19
  228.3 1.2 collective-permute-done.18
  230.4 3.4 collective-permute-done.19
  238.6 0.8 fusion.6
  239.7 0.8 copy.95
  240.6 1.9 collective-permute-start.20
  242.5 2.4 collective-permute-start.21
  245.7 1.4 divide_select_fusion.2
  247.3 0.8 copy_add_fusion
  248.2 3.6 scatter-add.54
  251.8 1.8 slice_add_fusion
  253.6 5.7 %scatter-add.55 = f32[16,40,128]{2,1,0:T(8,128)S(1)} dynamic-update-slice(f32[16,40,128]{2,1,0:T(8,128)S(1)} %scatter-add.54, f32[16,40,4]{2,1,0:T(8,128)} %slice_add_fusion, s32[]{:T(128)} %constant.298.clone.1, s32[]{:T(128)} %constant.298.clone.1, s32[]{:T(128)} %constant.301.clone.1) | dynamic-update-slice | bytes 20484 | tf_op jit(solution)/shard_map/scatter-add | solution.py:123
  259.4 3.4 collective-permute-start.22
  263.2 1.4 collective-permute-start.23
  264.7 4.6 %collective-permute-done.23 = f32[16,4,128]{2,1,0:T(4,128)S(1)} collective-permute-done((f32[16,4,128]{2,1,0:T(4,128)S(1)}, f32[16,4,128]{2,1,0:T(4,128)S(1)}, u32[]{:S(2)}, u32[]{:S(2)}) %collective-permute-start.23) | collective-permute-done | bytes 32800 | tf_op jit(solution)/shard_map/ppermute | solution.py:37
  269.4 1.0 multiply_reduce_fusion
  270.4 23.8 %all-reduce.8 = (f32[]{:T(128)}, f32[]{:T(128)}) all-reduce(f32[]{:T(128)} %get-tuple-element.150, f32[]{:T(128)} %get-tuple-element.149), channel_id=1, replica_groups=mesh['gy'=16,'gx'=32] {'gy'}, use_global_device_ids=true, to_apply=%region_15.16 | all-reduce | flops 2 | bytes 16 | tf_op jit(solution)/shard_map/psum | solution.py:17
  294.2 70.3 %all-reduce.6 = (f32[]{:T(128)}, f32[]{:T(128)}) all-reduce(f32[]{:T(128)} %get-tuple-element.162, f32[]{:T(128)} %get-tuple-element.163), channel_id=1, replica_groups=mesh['gy'=16,'gx'=32] {'gx'}, use_global_device_ids=true, to_apply=%region_16.17 | all-reduce | flops 2 | bytes 16 | tf_op jit(solution)/shard_map/psum | solution.py:17
  365.7 0.7 multiply_subtract_fusion
  (173 shorter events, 26.2 us)
Async XLA Ops:
  0.9 8.8 %collective-permute-start = (f32[16,4,128]{2,1,0:T(4,128)S(1)}, f32[16,4,128]{2,1,0:T(4,128)S(1)}, u32[]{:S(2)}, u32[]{:S(2)}) collective-permute-start(f32[16,4,128]{2,1,0:T(4,128)S(1)} %get-tuple-element.213), channel_id=1, source_target_pairs={{0,32},{32,64},{64,96},{96,128},{128,160},{160,192},{192,224},{224... | collective-permute-start | bytes 98312 | tf_op jit(solution)/shard_map/ppermute | solution.py:26
  5.3 4.8 %collective-permute-start.1 = (f32[16,4,128]{2,1,0:T(4,128)S(1)}, f32[16,4,128]{2,1,0:T(4,128)S(1)}, u32[]{:S(2)}, u32[]{:S(2)}) collective-permute-start(f32[16,4,128]{2,1,0:T(4,128)S(1)} %get-tuple-element.214), channel_id=1, source_target_pairs={{32,0},{64,32},{96,64},{128,96},{160,128},{192,160},{224,192},{256... | collective-permute-start | bytes 98312 | tf_op jit(solution)/shard_map/ppermute | solution.py:29
  6.7 0.7 copy-start.30
  6.7 2.1 copy-start.25
  6.8 3.3 copy-start
  8.8 25.2 %copy-start.31 = (pred[33]{0:T(512)(128)(4,1)}, pred[33]{0:T(512)(128)(4,1)S(1)}, u32[]{:S(2)}) copy-start(pred[33]{0:T(512)(128)(4,1)S(1)} %get-tuple-element.219) | copy-start | bytes 103
  8.8 42.6 %copy-start.26 = (pred[129]{0:T(512)(128)(4,1)}, pred[129]{0:T(512)(128)(4,1)S(1)}, u32[]{:S(2)}) copy-start(pred[129]{0:T(512)(128)(4,1)S(1)} %get-tuple-element.217) | copy-start | bytes 391
  9.2 16.1 %copy-start.19 = (f32[40,32]{0,1:T(8,128)}, f32[40,32]{0,1:T(8,128)S(1)}, u32[]{:S(2)}) copy-start(f32[40,32]{0,1:T(8,128)S(1)} %select_reduce_fusion.2) | copy-start | bytes 15364
  9.3 17.6 %copy-start.16 = (f32[32,40]{1,0:T(8,128)}, f32[32,40]{1,0:T(8,128)S(1)}, u32[]{:S(2)}) copy-start(f32[32,40]{1,0:T(8,128)S(1)} %select_reduce_fusion.3) | copy-start | bytes 15364
  9.5 16.8 %copy-start.7 = (f32[128,136]{0,1:T(8,128)}, f32[128,136]{0,1:T(8,128)S(1)}, u32[]{:S(2)}) copy-start(f32[128,136]{0,1:T(8,128)S(1)} %select_reduce_fusion) | copy-start | bytes 208900
  9.6 15.0 %copy-start.5 = (f32[136,128]{1,0:T(8,128)}, f32[136,128]{1,0:T(8,128)S(1)}, u32[]{:S(2)}) copy-start(f32[136,128]{1,0:T(8,128)S(1)} %select_reduce_fusion.1) | copy-start | bytes 208900
  10.1 13.7 %copy-start.11 = (f32[16,4,128]{2,1,0:T(4,128)}, f32[16,4,128]{2,1,0:T(4,128)S(1)}, u32[]{:S(2)}) copy-start(f32[16,4,128]{2,1,0:T(4,128)S(1)} %collective-permute-done.1) | copy-start | bytes 98308
  10.3 9.0 %collective-permute-start.2 = (f32[16,40,4]{2,1,0:T(8,128)S(1)}, f32[16,40,4]{2,1,0:T(8,128)S(1)}, u32[]{:S(2)}, u32[]{:S(2)}) collective-permute-start(f32[16,40,4]{2,1,0:T(8,128)S(1)} %get-tuple-element.207), channel_id=1, source_target_pairs={{0,1},{1,2},{2,3},{3,4},{4,5},{5,6},{6,7},{7,8},{8,9},{9,10},{10,1... | collective-permute-start | bytes 30728 | tf_op jit(solution)/shard_map/ppermute | solution.py:26
  15.4 10.3 %copy-start.22 = (f32[16,16]{1,0:T(8,128)}, f32[16,16]{1,0:T(8,128)S(1)}, u32[]{:S(2)}) copy-start(f32[16,16]{1,0:T(8,128)S(1)} %get-tuple-element.157) | copy-start | bytes 3076
  15.4 8.4 %collective-permute-start.3 = (f32[16,40,4]{2,1,0:T(8,128)S(1)}, f32[16,40,4]{2,1,0:T(8,128)S(1)}, u32[]{:S(2)}, u32[]{:S(2)}) collective-permute-start(f32[16,40,4]{2,1,0:T(8,128)S(1)} %get-tuple-element.208), channel_id=1, source_target_pairs={{1,0},{2,1},{3,2},{4,3},{5,4},{6,5},{7,6},{8,7},{9,8},{10,9},{11,1... | collective-permute-start | bytes 30728 | tf_op jit(solution)/shard_map/ppermute | solution.py:29
  29.5 4.5 %copy-start.12 = (f32[16,4,128]{2,1,0:T(4,128)S(1)}, f32[16,4,128]{2,1,0:T(4,128)}, u32[]{:S(2)}) copy-start(f32[16,4,128]{2,1,0:T(4,128)} %copy-done.11) | copy-start | bytes 98308
  29.6 5.9 %collective-permute-start.4 = (f32[16,40,4]{2,1,0:T(8,128)S(1)}, f32[16,40,4]{2,1,0:T(8,128)S(1)}, u32[]{:S(2)}, u32[]{:S(2)}) collective-permute-start(f32[16,40,4]{2,1,0:T(8,128)S(1)} %copy.86), channel_id=1, source_target_pairs={{0,1},{1,2},{2,3},{3,4},{4,5},{5,6},{6,7},{7,8},{8,9},{9,10},{10,1... | collective-permute-start | bytes 30728 | tf_op jit(solution)/shard_map/ppermute | solution.py:37
  31.6 8.7 %collective-permute-start.5 = (f32[16,40,4]{2,1,0:T(8,128)}, f32[16,40,4]{2,1,0:T(8,128)}, u32[]{:S(2)}, u32[]{:S(2)}) collective-permute-start(f32[16,40,4]{2,1,0:T(8,128)} %copy.87), channel_id=1, source_target_pairs={{1,0},{2,1},{3,2},{4,3},{5,4},{6,5},{7,6},{8,7},{9,8},{10,9},{11,1... | collective-permute-start | bytes 30728 | tf_op jit(solution)/shard_map/ppermute | solution.py:37
  47.8 3.6 copy-start.13
  47.9 5.3 %collective-permute-start.6 = (f32[16,4,128]{2,1,0:T(4,128)S(1)}, f32[16,4,128]{2,1,0:T(4,128)S(1)}, u32[]{:S(2)}, u32[]{:S(2)}) collective-permute-start(f32[16,4,128]{2,1,0:T(4,128)S(1)} %get-tuple-element.206), channel_id=1, source_target_pairs={{0,32},{32,64},{64,96},{96,128},{128,160},{160,192},{192,224},{224... | collective-permute-start | bytes 98312 | tf_op jit(solution)/shard_map/ppermute | solution.py:37
  51.9 6.0 %collective-permute-start.7 = (f32[16,4,128]{2,1,0:T(4,128)S(1)}, f32[16,4,128]{2,1,0:T(4,128)S(1)}, u32[]{:S(2)}, u32[]{:S(2)}) collective-permute-start(f32[16,4,128]{2,1,0:T(4,128)S(1)} %get-tuple-element.205), channel_id=1, source_target_pairs={{32,0},{64,32},{96,64},{128,96},{160,128},{192,160},{224,192},{256... | collective-permute-start | bytes 98312 | tf_op jit(solution)/shard_map/ppermute | solution.py:37
  59.0 6.2 %collective-permute-start.8 = (f32[16,4,128]{2,1,0:T(4,128)S(1)}, f32[16,4,128]{2,1,0:T(4,128)S(1)}, u32[]{:S(2)}, u32[]{:S(2)}) collective-permute-start(f32[16,4,128]{2,1,0:T(4,128)S(1)} %get-tuple-element.211), channel_id=1, source_target_pairs={{0,32},{32,64},{64,96},{96,128},{128,160},{160,192},{192,224},{224... | collective-permute-start | bytes 98312 | tf_op jit(solution)/shard_map/ppermute | solution.py:26
  63.9 4.7 %collective-permute-start.9 = (f32[16,4,128]{2,1,0:T(4,128)S(1)}, f32[16,4,128]{2,1,0:T(4,128)S(1)}, u32[]{:S(2)}, u32[]{:S(2)}) collective-permute-start(f32[16,4,128]{2,1,0:T(4,128)S(1)} %get-tuple-element.212), channel_id=1, source_target_pairs={{32,0},{64,32},{96,64},{128,96},{160,128},{192,160},{224,192},{256... | collective-permute-start | bytes 98312 | tf_op jit(solution)/shard_map/ppermute | solution.py:29
  68.5 26.6 %copy-start.14 = (f32[16,4,128]{2,1,0:T(4,128)}, f32[16,4,128]{2,1,0:T(4,128)S(1)}, u32[]{:S(2)}) copy-start(f32[16,4,128]{2,1,0:T(4,128)S(1)} %collective-permute-done.9) | copy-start | bytes 98308
  68.7 10.7 %collective-permute-start.10 = (f32[16,40,4]{2,1,0:T(8,128)S(1)}, f32[16,40,4]{2,1,0:T(8,128)S(1)}, u32[]{:S(2)}, u32[]{:S(2)}) collective-permute-start(f32[16,40,4]{2,1,0:T(8,128)S(1)} %get-tuple-element.203), channel_id=1, source_target_pairs={{0,1},{1,2},{2,3},{3,4},{4,5},{5,6},{6,7},{7,8},{8,9},{9,10},{10,1... | collective-permute-start | bytes 30728 | tf_op jit(solution)/shard_map/ppermute | solution.py:26
  75.5 8.4 %collective-permute-start.11 = (f32[16,40,4]{2,1,0:T(8,128)S(1)}, f32[16,40,4]{2,1,0:T(8,128)S(1)}, u32[]{:S(2)}, u32[]{:S(2)}) collective-permute-start(f32[16,40,4]{2,1,0:T(8,128)S(1)} %get-tuple-element.204), channel_id=1, source_target_pairs={{1,0},{2,1},{3,2},{4,3},{5,4},{6,5},{7,6},{8,7},{9,8},{10,9},{11,1... | collective-permute-start | bytes 30728 | tf_op jit(solution)/shard_map/ppermute | solution.py:29
  80.4 3.9 %copy-start.6 = (f32[136,128]{1,0:T(8,128)S(1)}, f32[136,128]{1,0:T(8,128)}, u32[]{:S(2)}) copy-start(f32[136,128]{1,0:T(8,128)} %copy-done.5) | copy-start | bytes 208900
  85.0 0.7 copy-start.20
  85.7 0.7 copy-start.23
  86.4 0.9 copy-start.8
  87.3 0.7 copy-start.17
  90.7 6.7 %collective-permute-start.12 = (f32[16,40,4]{2,1,0:T(8,128)S(1)}, f32[16,40,4]{2,1,0:T(8,128)S(1)}, u32[]{:S(2)}, u32[]{:S(2)}) collective-permute-start(f32[16,40,4]{2,1,0:T(8,128)S(1)} %copy.90), channel_id=1, source_target_pairs={{0,1},{1,2},{2,3},{3,4},{4,5},{5,6},{6,7},{7,8},{8,9},{9,10},{10,1... | collective-permute-start | bytes 30728 | tf_op jit(solution)/shard_map/ppermute | solution.py:37
  92.7 8.8 %collective-permute-start.13 = (f32[16,40,4]{2,1,0:T(8,128)}, f32[16,40,4]{2,1,0:T(8,128)}, u32[]{:S(2)}, u32[]{:S(2)}) collective-permute-start(f32[16,40,4]{2,1,0:T(8,128)} %copy.91), channel_id=1, source_target_pairs={{1,0},{2,1},{3,2},{4,3},{5,4},{6,5},{7,6},{8,7},{9,8},{10,9},{11,1... | collective-permute-start | bytes 30728 | tf_op jit(solution)/shard_map/ppermute | solution.py:37
  95.1 0.7 copy-start.27
  95.1 0.7 copy-start.32
  108.3 4.1 %copy-start.15 = (f32[16,4,128]{2,1,0:T(4,128)S(1)}, f32[16,4,128]{2,1,0:T(4,128)}, u32[]{:S(2)}) copy-start(f32[16,4,128]{2,1,0:T(4,128)} %copy-done.14) | copy-start | bytes 98308
  108.3 4.1 %copy-start.28 = (pred[129]{0:T(512)(128)(4,1)S(1)}, pred[129]{0:T(512)(128)(4,1)}, u32[]{:S(2)}) copy-start(pred[129]{0:T(512)(128)(4,1)} %copy-done.26) | copy-start | bytes 391
  108.3 6.0 %collective-permute-start.14 = (f32[16,4,128]{2,1,0:T(4,128)S(1)}, f32[16,4,128]{2,1,0:T(4,128)S(1)}, u32[]{:S(2)}, u32[]{:S(2)}) collective-permute-start(f32[16,4,128]{2,1,0:T(4,128)S(1)} %get-tuple-element.202), channel_id=1, source_target_pairs={{0,32},{32,64},{64,96},{96,128},{128,160},{160,192},{192,224},{224... | collective-permute-start | bytes 98312 | tf_op jit(solution)/shard_map/ppermute | solution.py:37
  112.7 5.3 %copy-start.4 = (f32[16,33,129]{2,1,0:T(8,128)S(1)}, f32[16,33,129]{2,1,0:T(8,128)}, u32[]{:S(2)}) copy-start(f32[16,33,129]{2,1,0:T(8,128)} %get-tuple-element.170) | copy-start | bytes 817348
  112.9 5.1 %copy-start.10 = (f32[16,32,128]{2,1,0:T(8,128)S(1)}, f32[16,32,128]{2,1,0:T(8,128)}, u32[]{:S(2)}) copy-start(f32[16,32,128]{2,1,0:T(8,128)} %get-tuple-element.173) | copy-start | bytes 786436
  112.9 5.1 %collective-permute-start.15 = (f32[16,4,128]{2,1,0:T(4,128)S(1)}, f32[16,4,128]{2,1,0:T(4,128)S(1)}, u32[]{:S(2)}, u32[]{:S(2)}) collective-permute-start(f32[16,4,128]{2,1,0:T(4,128)S(1)} %get-tuple-element.201), channel_id=1, source_target_pairs={{32,0},{64,32},{96,64},{128,96},{160,128},{192,160},{224,192},{256... | collective-permute-start | bytes 98312 | tf_op jit(solution)/shard_map/ppermute | solution.py:37
  119.1 98.0 %copy-start.1 = (f32[16,32,128]{2,1,0:T(8,128)}, f32[16,32,128]{2,1,0:T(8,128)S(1)}, u32[]{:S(2)}) copy-start(f32[16,32,128]{2,1,0:T(8,128)S(1)} %get-tuple-element.169) | copy-start | bytes 786436
  217.1 2.6 collective-permute-start.16
  218.4 4.9 %collective-permute-start.17 = (f32[16,4,128]{2,1,0:T(4,128)S(1)}, f32[16,4,128]{2,1,0:T(4,128)S(1)}, u32[]{:S(2)}, u32[]{:S(2)}) collective-permute-start(f32[16,4,128]{2,1,0:T(4,128)S(1)} %get-tuple-element.210), channel_id=1, source_target_pairs={{32,0},{64,32},{96,64},{128,96},{160,128},{192,160},{224,192},{256... | collective-permute-start | bytes 98312 | tf_op jit(solution)/shard_map/ppermute | solution.py:29
  223.5 5.9 %collective-permute-start.18 = (f32[16,40,4]{2,1,0:T(8,128)S(1)}, f32[16,40,4]{2,1,0:T(8,128)S(1)}, u32[]{:S(2)}, u32[]{:S(2)}) collective-permute-start(f32[16,40,4]{2,1,0:T(8,128)S(1)} %get-tuple-element.199), channel_id=1, source_target_pairs={{0,1},{1,2},{2,3},{3,4},{4,5},{5,6},{6,7},{7,8},{8,9},{9,10},{10,1... | collective-permute-start | bytes 30728 | tf_op jit(solution)/shard_map/ppermute | solution.py:26
  225.4 8.4 %collective-permute-start.19 = (f32[16,40,4]{2,1,0:T(8,128)S(1)}, f32[16,40,4]{2,1,0:T(8,128)S(1)}, u32[]{:S(2)}, u32[]{:S(2)}) collective-permute-start(f32[16,40,4]{2,1,0:T(8,128)S(1)} %get-tuple-element.200), channel_id=1, source_target_pairs={{1,0},{2,1},{3,2},{4,3},{5,4},{6,5},{7,6},{8,7},{9,8},{10,9},{11,1... | collective-permute-start | bytes 30728 | tf_op jit(solution)/shard_map/ppermute | solution.py:29
  234.9 0.7 copy-start.21
  235.6 0.7 copy-start.24
  236.3 0.9 copy-start.9
  237.2 0.7 copy-start.18
  240.6 6.7 %collective-permute-start.20 = (f32[16,40,4]{2,1,0:T(8,128)S(1)}, f32[16,40,4]{2,1,0:T(8,128)S(1)}, u32[]{:S(2)}, u32[]{:S(2)}) collective-permute-start(f32[16,40,4]{2,1,0:T(8,128)S(1)} %copy.94), channel_id=1, source_target_pairs={{0,1},{1,2},{2,3},{3,4},{4,5},{5,6},{6,7},{7,8},{8,9},{9,10},{10,1... | collective-permute-start | bytes 30728 | tf_op jit(solution)/shard_map/ppermute | solution.py:37
  242.5 9.2 %collective-permute-start.21 = (f32[16,40,4]{2,1,0:T(8,128)}, f32[16,40,4]{2,1,0:T(8,128)}, u32[]{:S(2)}, u32[]{:S(2)}) collective-permute-start(f32[16,40,4]{2,1,0:T(8,128)} %copy.95), channel_id=1, source_target_pairs={{1,0},{2,1},{3,2},{4,3},{5,4},{6,5},{7,6},{8,7},{9,8},{10,9},{11,1... | collective-permute-start | bytes 30728 | tf_op jit(solution)/shard_map/ppermute | solution.py:37
  245.0 0.7 copy-start.29
  245.0 0.7 copy-start.33
  259.4 5.3 %collective-permute-start.22 = (f32[16,4,128]{2,1,0:T(4,128)S(1)}, f32[16,4,128]{2,1,0:T(4,128)S(1)}, u32[]{:S(2)}, u32[]{:S(2)}) collective-permute-start(f32[16,4,128]{2,1,0:T(4,128)S(1)} %get-tuple-element.198), channel_id=1, source_target_pairs={{0,32},{32,64},{64,96},{96,128},{128,160},{160,192},{192,224},{224... | collective-permute-start | bytes 98312 | tf_op jit(solution)/shard_map/ppermute | solution.py:37
  263.0 6.3 %copy-start.3 = (f32[16,33,129]{2,1,0:T(8,128)S(1)}, f32[16,33,129]{2,1,0:T(8,128)}, u32[]{:S(2)}) copy-start(f32[16,33,129]{2,1,0:T(8,128)} %get-tuple-element.167) | copy-start | bytes 817348
  263.2 6.2 %copy-start.2 = (f32[16,32,128]{2,1,0:T(8,128)S(1)}, f32[16,32,128]{2,1,0:T(8,128)}, u32[]{:S(2)}) copy-start(f32[16,32,128]{2,1,0:T(8,128)} %copy-done.1) | copy-start | bytes 786436
  263.2 6.1 %collective-permute-start.23 = (f32[16,4,128]{2,1,0:T(4,128)S(1)}, f32[16,4,128]{2,1,0:T(4,128)S(1)}, u32[]{:S(2)}, u32[]{:S(2)}) collective-permute-start(f32[16,4,128]{2,1,0:T(4,128)S(1)} %get-tuple-element.197), channel_id=1, source_target_pairs={{32,0},{64,32},{96,64},{128,96},{160,128},{192,160},{224,192},{256... | collective-permute-start | bytes 98312 | tf_op jit(solution)/shard_map/ppermute | solution.py:37
